TPU v7x, 256 devices: a whole 4x4x8 slice. The times are simulated.
256 devices in a mesh: blk: 16 (over x_hi, z), wide: 16 (over y, x_lo, core).
Axes of the slice: x: 4 (x_hi: 2, x_lo: 2; x = x_hi * 2 + x_lo), y: 4, z: 8, core: 2. Of those that a mesh axis runs over, the one named last changes fastest.
Arguments:
- blocks: bfloat16 [4096, 64, 4096], P(('blk', 'wide')), may hold values from -24 to 24
- block_row: int32 [4096], P(('blk', 'wide')), may hold values from 0 to 3
- block_depth: int32 [4096], P(('blk', 'wide')), may hold values from 0 to 15
- live: int32 [4096], P(('blk', 'wide')), may hold values from 0 to 1, as said below
- factor_b: bfloat16 [1024, 256], P('blk'), may hold values from -6 to 6
- factor_c: bfloat16 [1024, 256], replicated, may hold values from -6 to 6
Outputs:
- factor_a: bfloat16 [4096, 256], P('wide')
- factor_b_new: bfloat16 [1024, 256], P(('blk', 'wide'))
Inputs may be any that keep to these rules, and one draw needn't show every extreme that they name: 1 marks a slot that holds a block, 0 an empty one; the share of live slots differs between devices, and slots 0 to 15 are all live.
All inputs are finite; a program needn't handle non-finite values.
Results may differ from a plain program's by a relative error of at most 0.0091.
Values may be sent and summed in bfloat16 or wider, within the bound.
A program may use at most 64 MiB of HBM per device.

v0:
```python
import jax
import jax.numpy as jnp
from jax import lax
from jax.sharding import PartitionSpec as P

BLOCK = 64
ROW_BLOCKS = 4
ROWS_C = 1024
RIDGE = 0.05


def factor_solve(partial_rows, gram):
    size = gram.shape[0]
    system = gram + RIDGE * jnp.eye(size, dtype=jnp.float32)
    lower = jnp.linalg.cholesky(system)
    solved = jax.scipy.linalg.cho_solve((lower, True), partial_rows.T)
    return solved.T * (0.125 / BLOCK)


def first_term(block, brows, crows):
    width = brows.shape[1]
    paired = (brows.astype(jnp.float32)[:, None, :] * crows.astype(jnp.float32)[None, :, :]).astype(
        jnp.bfloat16
    )
    return jnp.dot(block, paired.reshape(-1, width), preferred_element_type=jnp.float32)


def second_term(block, arows, crows):
    edge = arows.shape[0]
    paired = (arows.astype(jnp.float32)[:, None, :] * crows.astype(jnp.float32)[None, :, :]).astype(
        jnp.bfloat16
    )
    cube = block.reshape(edge, edge, edge)
    return lax.dot_general(
        cube, paired, (((0, 2), (0, 1)), ((), ())), preferred_element_type=jnp.float32
    )


def per_device(blocks, block_row, block_depth, live, factor_b, factor_c):
    edge = blocks.shape[1]
    slot_total = blocks.shape[0]
    rank = factor_c.shape[1]
    slice_rows = ROW_BLOCKS * BLOCK
    weights = live.astype(jnp.float32)
    gram_c = jnp.dot(factor_c.T, factor_c, preferred_element_type=jnp.float32) / ROWS_C
    empty_rows = jnp.zeros((slice_rows, rank), jnp.float32)
    gram_scale = lax.axis_size("blk") * edge
    piece = lax.all_gather(factor_b, "blk", axis=0, tiled=True)
    count = piece.shape[0] // edge

    def one_slot(step, acc):
        brows = lax.dynamic_slice_in_dim(piece, step * edge, edge, 0)
        crows = lax.dynamic_slice_in_dim(factor_c, block_depth[step] * edge, edge, 0)
        term = first_term(blocks[step], brows, crows) * weights[step]
        row = block_row[step] * edge
        current = lax.dynamic_slice_in_dim(acc, row, edge, 0)
        return lax.dynamic_update_slice_in_dim(acc, current + term, row, 0)

    mttkrp_part = lax.fori_loop(0, count, one_slot, empty_rows)
    panel_gram = jnp.dot(factor_b.T, factor_b, preferred_element_type=jnp.float32)
    gram_b = lax.psum(panel_gram, "blk") / gram_scale
    system_a = gram_c * gram_b
    total_rows = lax.axis_size("wide") * slice_rows
    mttkrp_a = lax.psum(mttkrp_part, "blk")
    factor_a = factor_solve(mttkrp_a, system_a).astype(jnp.bfloat16)
    slice_gram = jnp.dot(factor_a.T, factor_a, preferred_element_type=jnp.float32)
    gram_a = lax.psum(slice_gram, "wide") / total_rows

    def second_part(slot):
        arows = lax.dynamic_slice_in_dim(factor_a, block_row[slot] * edge, edge, 0)
        crows = lax.dynamic_slice_in_dim(factor_c, block_depth[slot] * edge, edge, 0)
        return second_term(blocks[slot], arows, crows) * weights[slot]

    partials = lax.map(second_part, jnp.arange(slot_total, dtype=jnp.int32))
    flat = partials.reshape(slot_total * edge, rank)
    mttkrp_b = lax.psum_scatter(flat, ("blk", "wide"), scatter_dimension=0, tiled=True)
    factor_b_new = factor_solve(mttkrp_b, gram_c * gram_a).astype(jnp.bfloat16)
    return (factor_a, factor_b_new)


def solution(mesh):
    in_specs = (
        P(("blk", "wide"), None, None),
        P(("blk", "wide")),
        P(("blk", "wide")),
        P(("blk", "wide")),
        P("blk", None),
        P(),
    )
    out_specs = (P("wide", None), P(("blk", "wide"), None))
    return jax.shard_map(
        per_device, mesh=mesh, in_specs=in_specs, out_specs=out_specs, check_vma=False
    )
```

profile of v0, /device:TPU:2, one launch (start us, length us, event | category | flops | bytes accessed | tf_op | source)
XLA Modules:
  0.0 851.8 jit_solution(16122719357660556276)
XLA Ops:
  7.2 46.3 %all_gather.3 = bf16[1024,256]{1,0:T(8,128)(2,1)S(1)} all-gather(bf16[64,256]{1,0:T(8,128)(2,1)} %param.15), channel_id=1, replica_groups=mesh['blk'=16,'wide'=16] {'blk'}, dimensions={0}, use_global_device_ids=true | all-gather | bytes 557056 | tf_op jit(solution)/shard_map/all_gather | solution.py:48
  56.0 134.5 %while.25 = (s32[]{:T(128)}, f32[256,256]{1,0:T(8,128)S(1)}, s32[16]{0:T(128)}, bf16[16,64,4096]{2,1,0:T(8,128)(2,1)}, bf16[1024,256]{1,0:T(8,128)(2,1)S(1)}, /*...) while((s32[]{:T(128)}, f32[256,256]{1,0:T(8,128)S(1)}, ...), condition=%wide.region_6.8_spmd, body=%wide.region_5.7_spmd.sunk | while | flops 136380432 | bytes 5178687 | solution.py:59
  62.2 2.2 fusion.74
  70.6 2.2 fusion.74
  79.0 2.2 fusion.74
  87.4 2.2 fusion.74
  95.8 2.2 fusion.74
  104.2 2.2 fusion.74
  112.6 2.2 fusion.74
  121.0 2.2 fusion.74
  129.5 2.2 fusion.74
  137.9 2.2 fusion.74
  146.3 2.2 fusion.74
  154.7 2.2 fusion.74
  163.1 2.2 fusion.74
  171.5 2.2 fusion.74
  179.9 2.2 fusion.74
  188.3 2.2 fusion.74
  191.3 152.3 %all-reduce.11.cloned.1.call-done = (f32[256,256]{0,1:T(8,128)}, f32[256,256]{0,1:T(8,128)}) async-done(((f32[256,256]{0,1:T(8,128)}, f32[256,256]{0,1:T(8,128)}), (f32[256,256]{0,1:T(8,128)}, f32[256,256]{0,1:T(8,128)})) %all-reduce.11.cloned.1.call-update) | async-done | bytes 524304 | tf_op jit(solution)/shard_map/psum | solution.py:64
  343.6 1.8 select_add_fusion.1
  345.6 11.7 %cholesky.130 = f32[128,128]{1,0:T(8,128)S(1)} custom-call(f32[128,128]{1,0:T(8,128)S(1)} %cholesky.194), custom_call_target="Cholesky" | custom-call | tf_op jit(solution)/shard_map/jit(cholesky)/cholesky | solution.py:15
  357.4 9.8 %custom-call.25 = f32[1,128,128]{1,2,0:T(8,128)S(1)} custom-call(f32[1,128,128]{2,1,0:T(8,128)S(1)} %get-tuple-element.324), custom_call_target="InvertDiagBlocksLowerTriangular" | custom-call | tf_op jit(solution)/shard_map/jit(cholesky)/cholesky | solution.py:15
  367.7 11.7 %cholesky.147 = f32[128,128]{1,0:T(8,128)S(1)} custom-call(f32[128,128]{1,0:T(8,128)S(1)} %convolution_subtract_fusion.3), custom_call_target="Cholesky" | custom-call | tf_op jit(solution)/shard_map/jit(cholesky)/cholesky | solution.py:15
  381.9 4.4 while.27
  386.3 19.7 %custom-call.22 = f32[2,128,128]{1,2,0:T(8,128)S(1)} custom-call(f32[2,128,128]{2,1,0:T(8,128)S(1)} %get-tuple-element.198), custom_call_target="InvertDiagBlocksLowerTriangular" | custom-call | tf_op jit(solution)/shard_map/jit(_cho_solve)/triangular_solve | solution.py:16
  409.0 176.0 %while.26 = (s32[]{:T(128)}, f32[16,64,256]{2,1,0:T(8,128)}, s32[16]{0:T(128)S(1)}, bf16[16,64,4096]{2,1,0:T(8,128)(2,1)}, s32[16]{0:T(128)S(1)}, /*index=5*/bf1...) while((s32[]{:T(128)}, f32[16,64,256]{2,1,0:T(8,128)}, ...), condition=%wide.region_10.12_spmd, body=%wide.region_9.11_spmd.sunk | while | flops 136364048 | bytes 3016007 | solution.py:74
  418.1 1.9 fusion.76
  429.1 1.9 fusion.76
  440.1 1.9 fusion.76
  451.1 1.9 fusion.76
  462.1 1.9 fusion.76
  473.1 1.9 fusion.76
  484.1 1.9 fusion.76
  495.1 1.9 fusion.76
  506.1 1.9 fusion.76
  517.1 1.9 fusion.76
  528.1 1.9 fusion.76
  539.1 1.9 fusion.76
  550.1 1.9 fusion.76
  561.0 1.9 fusion.76
  572.0 1.9 fusion.76
  583.0 1.9 fusion.76
  586.2 11.7 %cholesky.164 = f32[128,128]{1,0:T(8,128)S(1)} custom-call(f32[128,128]{1,0:T(8,128)S(1)} %cholesky.197), custom_call_target="Cholesky" | custom-call | tf_op jit(solution)/shard_map/jit(cholesky)/cholesky | solution.py:15
  597.9 9.8 %custom-call.26 = f32[1,128,128]{1,2,0:T(8,128)S(1)} custom-call(f32[1,128,128]{2,1,0:T(8,128)S(1)} %get-tuple-element.322), custom_call_target="InvertDiagBlocksLowerTriangular" | custom-call | tf_op jit(solution)/shard_map/jit(cholesky)/cholesky | solution.py:15
  608.2 11.7 %cholesky.181 = f32[128,128]{1,0:T(8,128)S(1)} custom-call(f32[128,128]{1,0:T(8,128)S(1)} %convolution_subtract_fusion.2), custom_call_target="Cholesky" | custom-call | tf_op jit(solution)/shard_map/jit(cholesky)/cholesky | solution.py:15
  622.9 4.3 while.28
  627.3 19.7 %custom-call.23 = f32[2,128,128]{1,2,0:T(8,128)S(1)} custom-call(f32[2,128,128]{2,1,0:T(8,128)S(1)} %get-tuple-element.206), custom_call_target="InvertDiagBlocksLowerTriangular" | custom-call | tf_op jit(solution)/shard_map/jit(_cho_solve)/triangular_solve | solution.py:16
  646.9 195.7 %all-reduce.9.cloned.1.call-done = f32[1024,256]{1,0:T(8,128)} async-done(((f32[1024,256]{1,0:T(8,128)}), f32[1024,256]{1,0:T(8,128)}) %all-reduce.9.cloned.1.call-update) | async-done | bytes 1048592
  (287 shorter events, 188.8 us)
Async XLA Ops:
  7.2 336.4 %all-reduce.11.cloned.1.call-start = ((), (), s32[]{:S(2)}) async-start(), calls=%async_computation.2 | async-start | bytes 1048576 | tf_op jit(solution)/shard_map/psum | solution.py:64
  190.5 0.7 copy-start
  191.3 393.7 %all-reduce.7.cloned.1.call-start = ((), (), s32[]{:S(2)}) async-start(), calls=%async_computation | async-start | bytes 524288 | tf_op jit(solution)/shard_map/psum | solution.py:67
  343.6 62.3 %copy-start.2 = (f32[256,256]{0,1:T(8,128)S(1)}, f32[256,256]{0,1:T(8,128)}, u32[]{:S(2)}) copy-start(f32[256,256]{0,1:T(8,128)} %get-tuple-element.311) | copy-start | bytes 786436
  345.6 63.3 %copy-start.3 = (s32[16]{0:T(128)S(1)}, s32[16]{0:T(128)}, u32[]{:S(2)}) copy-start(s32[16]{0:T(128)} %get-tuple-element.639) | copy-start | bytes 196
  345.6 63.3 %copy-start.4 = (s32[16]{0:T(128)S(1)}, s32[16]{0:T(128)}, u32[]{:S(2)}) copy-start(s32[16]{0:T(128)} %get-tuple-element.640) | copy-start | bytes 196
  408.8 433.9 %all-reduce.9.cloned.1.call-start = ((), (), s32[]{:S(2)}) async-start(), calls=%async_computation.1 | async-start | bytes 2097152
  584.9 260.4 %copy-start.1 = (bf16[256,256]{1,0:T(8,128)(2,1)}, bf16[256,256]{1,0:T(8,128)(2,1)S(1)}, u32[]{:S(2)}) copy-start(bf16[256,256]{1,0:T(8,128)(2,1)S(1)} %get-tuple-element.633) | copy-start | bytes 393220
Sparse Core Ops, SparseCore 0:
  191.4 152.1 all-reduce.10
  408.9 118.2 all-reduce.6
  585.1 257.5 all-reduce.8
where the time goes:
time: 858 us; the launch traced here: 852 us
  waiting for transfers between devices  348 us (41%)
  other arithmetic  146 us (17%)
  local copies, waits for them, and re-layouts  142 us (17%)
  loops' own time  79.6 us (9%)
  matrix products  73.4 us (9%)
  blocking collectives  46.3 us (5%)
  between operations  16.6 us (2%)
    unnamed x4, waiting for transfers between devices  196 us
    psum x1, waiting for transfers between devices, per_device(): mttkrp_a = lax.psum(mttkrp_part, 'blk')  152 us
    another operation x13, other arithmetic, factor_solve(): lower = jnp.linalg.cholesky(system)  68.6 us
    another operation x1, loops' own time, per_device(): partials = lax.map(second_part, jnp.arange(slot_total, dtype=jnp.int32))  55.9 us
    all_gather x1, blocking collectives, per_device(): piece = lax.all_gather(factor_b, 'blk', axis=0, tiled=True)  46.3 us
    another operation x5, other arithmetic, factor_solve(): solved = jax.scipy.linalg.cho_solve((lower, True), partial_rows.T)  39.4 us
    dot_general x16, matrix products, first_term(): jnp.dot(block, paired.reshape(-1, width), preferred_element_type=jnp.floa...  35.1 us
    dot_general x16, matrix products, second_term(): lax.dot_general(cube, paired, (((0, 2), (0, 1)), ((), ())), preferred_ele...  29.8 us
  transfers between devices with their start and end apart: 3, of which 2 were waited for; matrix products, arithmetic and copies ran while one was open for 21% of the time, Pallas kernels for 0%

commit v1 on v0

--- a/solution.py
+++ b/solution.py
@@ -61,7 +61,7 @@
     gram_b = lax.psum(panel_gram, "blk") / gram_scale
     system_a = gram_c * gram_b
     total_rows = lax.axis_size("wide") * slice_rows
-    mttkrp_a = lax.psum(mttkrp_part, "blk")
+    mttkrp_a = jnp.sum(lax.all_gather(mttkrp_part, "blk"), axis=0)
     factor_a = factor_solve(mttkrp_a, system_a).astype(jnp.bfloat16)
     slice_gram = jnp.dot(factor_a.T, factor_a, preferred_element_type=jnp.float32)
     gram_a = lax.psum(slice_gram, "wide") / total_rows

time: 858 us -> 740 us (0.86)
  waiting for transfers between devices: 348 us -> 228 us
    psum x1, waiting for transfers between devices: 152 us -> 0.02 us  [per_device(): gram_b = lax.psum(panel_gram, 'blk') / gram_scale]
    all_gather x0 -> x1, waiting for transfers between devices: none -> 32.5 us  [per_device(): mttkrp_a = jnp.sum(lax.all_gather(mttkrp_part, 'blk'), axis=0)]
    unnamed x4 -> x5, waiting for transfers between devices: 196 us -> 195 us
  transfers between devices with their start and end apart: 3 -> 4, of which waited for: 2 -> 2; matrix products, arithmetic and copies ran while one was open for 21% -> 48% of each run, Pallas kernels for 0% -> 0%
where the time goes in v1:
time: 740 us; the launch traced here: 734 us
  waiting for transfers between devices  228 us (31%)
  other arithmetic  149 us (20%)
  local copies, waits for them, and re-layouts  142 us (19%)
  loops' own time  79.5 us (11%)
  matrix products  73.3 us (10%)
  blocking collectives  46.4 us (6%)
  between operations  16.7 us (2%)
    unnamed x5, waiting for transfers between devices  195 us
    another operation x13, other arithmetic, factor_solve(): lower = jnp.linalg.cholesky(system)  68.7 us
    another operation x1, loops' own time, per_device(): partials = lax.map(second_part, jnp.arange(slot_total, dtype=jnp.int32))  55.8 us
    all_gather x1, blocking collectives, per_device(): piece = lax.all_gather(factor_b, 'blk', axis=0, tiled=True)  46.4 us
    another operation x5, other arithmetic, factor_solve(): solved = jax.scipy.linalg.cho_solve((lower, True), partial_rows.T)  39.4 us
    dot_general x16, matrix products, first_term(): jnp.dot(block, paired.reshape(-1, width), preferred_element_type=jnp.floa...  35.2 us
    all_gather x1, waiting for transfers between devices, per_device(): mttkrp_a = jnp.sum(lax.all_gather(mttkrp_part, 'blk'), axis=0)  32.5 us
    dot_general x16, matrix products, second_term(): lax.dot_general(cube, paired, (((0, 2), (0, 1)), ((), ())), preferred_ele...  29.7 us
  transfers between devices with their start and end apart: 4, of which 2 were waited for; matrix products, arithmetic and copies ran while one was open for 48% of the time, Pallas kernels for 0%

profile of v1, /device:TPU:2, one launch (start us, length us, event | category | flops | bytes accessed | tf_op | source)
XLA Modules:
  0.0 734.0 jit_solution(8826509394797026242)
XLA Ops:
  9.1 46.4 %all_gather.9 = bf16[1024,256]{1,0:T(8,128)(2,1)S(1)} all-gather(bf16[64,256]{1,0:T(8,128)(2,1)} %param.15), channel_id=1, replica_groups=mesh['blk'=16,'wide'=16] {'blk'}, dimensions={0}, use_global_device_ids=true | all-gather | bytes 557056 | tf_op jit(solution)/shard_map/all_gather | solution.py:48
  56.1 134.6 %while.25 = (s32[]{:T(128)}, f32[256,256]{1,0:T(8,128)S(1)}, s32[16]{0:T(128)}, bf16[16,64,4096]{2,1,0:T(8,128)(2,1)}, bf16[1024,256]{1,0:T(8,128)(2,1)S(1)}, /*...) while((s32[]{:T(128)}, f32[256,256]{1,0:T(8,128)S(1)}, ...), condition=%wide.region_6.8_spmd, body=%wide.region_5.7_spmd.sunk | while | flops 136380432 | bytes 5178187 | solution.py:59
  62.3 2.2 fusion.74
  70.8 2.2 fusion.74
  79.2 2.2 fusion.74
  87.6 2.2 fusion.74
  96.0 2.2 fusion.74
  104.4 2.2 fusion.74
  112.8 2.2 fusion.74
  121.2 2.2 fusion.74
  129.7 2.2 fusion.74
  138.1 2.2 fusion.74
  146.5 2.2 fusion.74
  154.9 2.2 fusion.74
  163.3 2.2 fusion.74
  171.7 2.2 fusion.74
  180.1 2.2 fusion.74
  188.5 2.2 fusion.74
  193.5 11.7 %cholesky.130 = f32[128,128]{1,0:T(8,128)S(1)} custom-call(f32[128,128]{1,0:T(8,128)S(1)} %cholesky.194), custom_call_target="Cholesky" | custom-call | tf_op jit(solution)/shard_map/jit(cholesky)/cholesky | solution.py:15
  205.3 9.8 %custom-call.25 = f32[1,128,128]{1,2,0:T(8,128)S(1)} custom-call(f32[1,128,128]{2,1,0:T(8,128)S(1)} %get-tuple-element.322), custom_call_target="InvertDiagBlocksLowerTriangular" | custom-call | tf_op jit(solution)/shard_map/jit(cholesky)/cholesky | solution.py:15
  215.7 11.7 %cholesky.147 = f32[128,128]{1,0:T(8,128)S(1)} custom-call(f32[128,128]{1,0:T(8,128)S(1)} %convolution_subtract_fusion.3), custom_call_target="Cholesky" | custom-call | tf_op jit(solution)/shard_map/jit(cholesky)/cholesky | solution.py:15
  229.7 4.3 while.27
  234.0 19.7 %custom-call.22 = f32[2,128,128]{1,2,0:T(8,128)S(1)} custom-call(f32[2,128,128]{2,1,0:T(8,128)S(1)} %get-tuple-element.198), custom_call_target="InvertDiagBlocksLowerTriangular" | custom-call | tf_op jit(solution)/shard_map/jit(_cho_solve)/triangular_solve | solution.py:16
  253.7 32.5 %all-gather.3.cloned.1.call-done = f32[4096,256]{1,0:T(8,128)} async-done(((f32[256,256]{1,0:T(8,128)}), f32[4096,256]{1,0:T(8,128)}) %all-gather.3.cloned.1.call-update) | async-done | bytes 4194320 | tf_op jit(solution)/shard_map/all_gather | solution.py:64
  286.2 2.5 reduce_sum.9
  291.7 176.0 %while.26 = (s32[]{:T(128)}, f32[16,64,256]{2,1,0:T(8,128)}, s32[16]{0:T(128)S(1)}, bf16[16,64,4096]{2,1,0:T(8,128)(2,1)}, s32[16]{0:T(128)S(1)}, /*index=5*/bf1...) while((s32[]{:T(128)}, f32[16,64,256]{2,1,0:T(8,128)}, ...), condition=%wide.region_10.12_spmd, body=%wide.region_9.11_spmd.sunk | while | flops 136364048 | bytes 3015507 | solution.py:74
  300.8 1.9 fusion.76
  311.9 1.9 fusion.76
  322.9 1.9 fusion.76
  333.9 1.9 fusion.76
  344.9 1.9 fusion.76
  355.8 1.9 fusion.76
  366.8 1.9 fusion.76
  377.8 1.9 fusion.76
  388.8 1.9 fusion.76
  399.8 1.9 fusion.76
  410.8 1.9 fusion.76
  421.8 1.9 fusion.76
  432.8 1.9 fusion.76
  443.8 1.9 fusion.76
  454.8 1.9 fusion.76
  465.8 1.9 fusion.76
  468.9 11.7 %cholesky.164 = f32[128,128]{1,0:T(8,128)S(1)} custom-call(f32[128,128]{1,0:T(8,128)S(1)} %cholesky.197), custom_call_target="Cholesky" | custom-call | tf_op jit(solution)/shard_map/jit(cholesky)/cholesky | solution.py:15
  480.8 9.8 %custom-call.26 = f32[1,128,128]{1,2,0:T(8,128)S(1)} custom-call(f32[1,128,128]{2,1,0:T(8,128)S(1)} %get-tuple-element.320), custom_call_target="InvertDiagBlocksLowerTriangular" | custom-call | tf_op jit(solution)/shard_map/jit(cholesky)/cholesky | solution.py:15
  491.2 11.7 %cholesky.181 = f32[128,128]{1,0:T(8,128)S(1)} custom-call(f32[128,128]{1,0:T(8,128)S(1)} %convolution_subtract_fusion.2), custom_call_target="Cholesky" | custom-call | tf_op jit(solution)/shard_map/jit(cholesky)/cholesky | solution.py:15
  505.7 4.5 while.28
  510.3 19.7 %custom-call.23 = f32[2,128,128]{1,2,0:T(8,128)S(1)} custom-call(f32[2,128,128]{2,1,0:T(8,128)S(1)} %get-tuple-element.206), custom_call_target="InvertDiagBlocksLowerTriangular" | custom-call | tf_op jit(solution)/shard_map/jit(_cho_solve)/triangular_solve | solution.py:16
  530.0 194.9 %all-reduce.10.cloned.1.call-done = f32[1024,256]{1,0:T(8,128)} async-done(((f32[1024,256]{1,0:T(8,128)}), f32[1024,256]{1,0:T(8,128)}) %all-reduce.10.cloned.1.call-update) | async-done | bytes 1048592
  (289 shorter events, 190.8 us)
Async XLA Ops:
  7.2 184.4 %all-reduce.6.cloned.1.call-start = ((), (), s32[]{:S(2)}) async-start(), calls=%async_computation | async-start | bytes 524288 | tf_op jit(solution)/shard_map/psum | solution.py:61
  9.0 277.2 %all-gather.3.cloned.1.call-start = ((), (), s32[]{:S(2)}) async-start(), calls=%async_computation.2 | async-start | bytes 4456448 | tf_op jit(solution)/shard_map/all_gather | solution.py:64
  190.8 0.7 copy-start
  191.5 276.2 %all-reduce.8.cloned.1.call-start = ((), (), s32[]{:S(2)}) async-start(), calls=%async_computation.1 | async-start | bytes 524288 | tf_op jit(solution)/shard_map/psum | solution.py:67
  233.9 57.7 %copy-start.2 = (s32[16]{0:T(128)S(1)}, s32[16]{0:T(128)}, u32[]{:S(2)}) copy-start(s32[16]{0:T(128)} %get-tuple-element.635) | copy-start | bytes 196
  234.0 57.7 %copy-start.3 = (s32[16]{0:T(128)S(1)}, s32[16]{0:T(128)}, u32[]{:S(2)}) copy-start(s32[16]{0:T(128)} %get-tuple-element.636) | copy-start | bytes 196
  291.6 433.2 %all-reduce.10.cloned.1.call-start = ((), (), s32[]{:S(2)}) async-start(), calls=%async_computation.3 | async-start | bytes 2097152
  467.7 259.8 %copy-start.1 = (bf16[256,256]{1,0:T(8,128)(2,1)}, bf16[256,256]{1,0:T(8,128)(2,1)S(1)}, u32[]{:S(2)}) copy-start(bf16[256,256]{1,0:T(8,128)(2,1)S(1)} %get-tuple-element.631) | copy-start | bytes 393220
Sparse Core Ops, SparseCore 0:
  10.6 159.0 all-reduce.5
  191.6 94.5 all-gather.2
  291.7 117.6 all-reduce.7
  467.8 256.9 all-reduce.9
